TPU v7x, 256 devices: a whole 4x4x8 slice. The times are simulated.
256 devices in a mesh: lon: 16 (over y_lo, z), lat: 16 (over x, y_hi, core).
Axes of the slice: x: 4, y: 4 (y_hi: 2, y_lo: 2; y = y_hi * 2 + y_lo), z: 8, core: 2. Of those that a mesh axis runs over, the one named last changes fastest.
Arguments:
- crosswise_speed_units: float32 [8, 256, 4096], P(None, 'lat', 'lon'), may hold values from -6 to 6
- poleward_speed_units: float32 [8, 256, 4096], P(None, 'lat', 'lon'), may hold values from -6 to 6
- thermal_anomaly: float32 [8, 256, 4096], P(None, 'lat', 'lon'), may hold values from -6 to 6
- saltiness_anomaly: float32 [8, 256, 4096], P(None, 'lat', 'lon'), may hold values from -6 to 6
- freeboard_elevation: float32 [256, 4096], P('lat', 'lon'), may hold values from -6 to 6
- barotropic_zonal_flow: float32 [256, 4096], P('lat', 'lon'), may hold values from -6 to 6
- barotropic_meridional_flow: float32 [256, 4096], P('lat', 'lon'), may hold values from -6 to 6
- submerged_layer_tally: int32 [256, 4096], P('lat', 'lon'), may hold values from 0 to 8
- seam_partner_index: int32 [4096], P('lon'), may hold values from 0 to 4095, as said below
Outputs:
- zonal_speed_final: float32 [8, 256, 4096], P(None, 'lat', 'lon')
- poleward_speed_final: float32 [8, 256, 4096], P(None, 'lat', 'lon')
- thermal_final: float32 [8, 256, 4096], P(None, 'lat', 'lon')
- saltiness_final: float32 [8, 256, 4096], P(None, 'lat', 'lon')
- freeboard_final: float32 [256, 4096], P('lat', 'lon')
- barotropic_zonal_final: float32 [256, 4096], P('lat', 'lon')
- barotropic_meridional_final: float32 [256, 4096], P('lat', 'lon')
Inputs may be any that keep to these rules, and one draw needn't show every extreme that they name: seam_partner_index[seam_partner_index[c]] = c, and seam_partner_index[(c + 1) mod 4096] = (seam_partner_index[c] - 1) mod 4096 for every column c.
All inputs are finite; a program needn't handle non-finite values.
Results may differ from a plain program's by a relative error of at most 0.0003.
Values sent between devices are 32-bit elements; how exact they have to be, the bound alone decides.
A program may use at most 128 MiB of HBM per device.

v0:
```python
import functools

import jax
import jax.numpy as jnp
from jax import lax
from jax.experimental import pallas as pl
from jax.experimental.pallas import tpu as pltpu
from jax.sharding import PartitionSpec as P

MESH = pl.DeviceIdType.MESH

SUBSTEPS = 12
COURANT = 0.15
PRESSURE_GAIN = 0.1
CORIOLIS = 0.3
WAVE_MASS = 1.2
WAVE_MOMENTUM = 1.2
EPSILON = 1e-06

LEVELS, ROWS, COLS = 8, 16, 256
MARGIN = 2 * SUBSTEPS
WIDE = ROWS + 2 * MARGIN
LANES = 128

SEA, ZON, MER, TALLY, MEANZ, MEANM = range(6)


def weno_flux(em2, em1, e0, ep1, ep2, q0, q1, carry, drift, ahead):
    far = jnp.where(ahead, em2, ep2)
    near = jnp.where(ahead, em1, ep1)
    down = jnp.where(ahead, ep1, em1)
    centre = jnp.where(ahead, q0, q1)
    b0 = far * (4.0 * far - 11.0 * near) + (10.0 * near * near + 3.0 * EPSILON)
    b1 = near * (4.0 * near - 5.0 * e0) + (4.0 * e0 * e0 + 3.0 * EPSILON)
    b2 = e0 * (10.0 * e0 - 11.0 * down) + (4.0 * down * down + 3.0 * EPSILON)
    m0 = b1 * b2
    m1 = b0 * b2
    m2 = b0 * b1
    s0 = m0 * m0
    s1 = 6.0 * (m1 * m1)
    s2 = 3.0 * (m2 * m2)
    top = s0 * (5.0 * near - 2.0 * far) + s1 * (near + 2.0 * e0) + s2 * (4.0 * e0 - down)
    return carry * centre + drift * (top / (s0 + s1 + s2))


def wrapped(value, size):
    return lax.rem(value + 2 * size, size)


def turner(seam_ref):
    lane = lax.broadcasted_iota(jnp.int32, (LEVELS, LANES), 1)
    level = lax.broadcasted_iota(jnp.int32, (LEVELS, LANES), 0)
    first_partner = jnp.full((LEVELS, LANES), seam_ref[0], jnp.int32)
    upper = jnp.bitwise_and(first_partner, LANES) != 0
    base = jnp.bitwise_and(first_partner, LANES - 1)
    picked = jnp.bitwise_and(base - lane, LANES - 1)

    def turn_lanes(low, high):
        return jnp.take_along_axis(jnp.where(upper, high, low), picked, axis=1)

    mirror = LEVELS - 1 - level

    def flip_rows(x):
        return jnp.take_along_axis(x, mirror, axis=0)

    return turn_lanes, flip_rows, lane <= base


def pack_margins(tiles):
    lane = lax.broadcasted_iota(jnp.int32, (LEVELS, LANES), 1)
    group = lax.shift_right_logical(lane * 43, 10)
    west = jnp.zeros((LEVELS, LANES), jnp.float32)
    east = west
    for g, (first, last) in enumerate(tiles):
        if g:
            first = pltpu.roll(first, MARGIN * g, 1)
        last = pltpu.roll(last, (MARGIN * g + MARGIN) % LANES, 1)
        west = jnp.where(group == g, first, west)
        east = jnp.where(group == g, last, east)
    return west, east


def prepare(
    u_in, v_in, t_in, s_in, sea_in, zon_in, mer_in, tally_in, cells, edges, rim, margins,
    raw, tally_raw, flat, sems
):
    f32 = jnp.float32
    loads = [pltpu.make_async_copy(tally_in, tally_raw, sems.at[11])]
    for f, ref in enumerate((u_in, v_in, t_in, s_in)):
        for t in range(2):
            lanes = slice(t * LANES, (t + 1) * LANES)
            loads.append(pltpu.make_async_copy(ref.at[:, lanes], raw.at[f, t], sems.at[2 * f + t]))
    for f, ref in enumerate((sea_in, zon_in, mer_in)):
        loads.append(pltpu.make_async_copy(ref, rim.at[f], sems.at[8 + f]))
    for copy in loads:
        copy.start()
    for copy in loads:
        copy.wait()
    level = lax.broadcasted_iota(jnp.int32, (LEVELS, LANES), 0).astype(f32)
    lane = lax.broadcasted_iota(jnp.int32, (LEVELS, LANES), 1)
    for t in range(2):
        lanes = slice(t * LANES, (t + 1) * LANES)
        tally = tally_raw[:, lanes].astype(f32)
        rim[TALLY, :, lanes] = tally
        flat[t] = tally
    for pair in range(2):
        tiles = [
            (
                rim[2 * pair + g // 2, 8 * (g % 2) : 8 * (g % 2) + 8, 0:LANES],
                rim[2 * pair + g // 2, 8 * (g % 2) : 8 * (g % 2) + 8, LANES:COLS],
            )
            for g in range(4)
        ]
        margins[0, pair], margins[1, pair] = pack_margins(tiles)
    triple = lax.shift_right_logical(lane * 43, 7)
    for n in range(2):
        for f in range(5):
            edges[n, f] = jnp.zeros((LEVELS, LANES), f32)

    def arrange(r, _):
        mine = triple == r
        for f in range(5):
            tiles = []
            for t in range(2):
                if f < 4:
                    tile = raw[f, t, pl.ds(r, LEVELS, stride=ROWS), :]
                else:
                    tile = jnp.where(level < flat[t, pl.ds(r, 1), :], 1.0, 0.0)
                cells[f, r, t] = tile
                tiles.append(tile)
            edges[0, f] = jnp.where(mine, pltpu.roll(tiles[0], 3 * r, 1), edges[0, f])
            edges[1, f] = jnp.where(mine, pltpu.roll(tiles[1], 3 * r + 3, 1), edges[1, f])
        return _

    lax.fori_loop(0, ROWS, arrange, 0)


def prepare_call(*arguments):
    f32 = jnp.float32
    vmem = pl.BlockSpec(memory_space=pltpu.VMEM)
    anywhere = pl.BlockSpec(memory_space=pl.ANY)
    return pl.pallas_call(
        prepare,
        out_shape=(
            jax.ShapeDtypeStruct((5, ROWS, 2, LEVELS, LANES), f32),
            jax.ShapeDtypeStruct((2, 5, LEVELS, LANES), f32),
            jax.ShapeDtypeStruct((4, ROWS, COLS), f32),
            jax.ShapeDtypeStruct((2, 2, LEVELS, LANES), f32),
        ),
        in_specs=[anywhere] * 8,
        out_specs=(vmem,) * 4,
        scratch_shapes=[
            pltpu.VMEM((4, 2, LEVELS * ROWS, LANES), f32),
            pltpu.VMEM((ROWS, COLS), jnp.int32),
            pltpu.VMEM((2, ROWS, LANES), f32),
            pltpu.SemaphoreType.DMA((12,)),
        ],
        name="prepare",
    )(*arguments)


class Links:
    SHIFTS = [(a, b) for a in (1, -1, 2, -2, 0) for b in (0, 1, -1) if (a, b) != (0, 0)]

    def __init__(self, lon_size, lat_size, turn=None):
        self.lon = lax.axis_index("lon")
        self.lat = lax.axis_index("lat")
        self.lon_size, self.lat_size, self.turn = lon_size, lat_size, turn
        self.top = self.lat == lat_size - 1
        self.below = self.lat == lat_size - 2
        self.barrier = pltpu.get_barrier_semaphore()

    def fold_peer(self, s):
        return wrapped(self.turn - self.lon + s - 2, self.lon_size)

    def lat_ok(self, a):
        return jnp.logical_and(self.lat + a >= 0, self.lat + a <= self.lat_size - 1)

    def when_lat(self, a, body):
        if a == 0:
            body()
        else:
            pl.when(self.lat_ok(a))(body)

    def peer(self, a, b):
        return {"lat": self.lat + a, "lon": wrapped(self.lon + b, self.lon_size)}

    def greet(self, to):
        pl.semaphore_signal(self.barrier, inc=1, device_id=to, device_id_type=MESH)

    def meet(self, shifts, top_slots=(), below_slots=()):
        count = jnp.int32(0)
        for a, b in shifts:
            self.when_lat(a, lambda a=a, b=b: self.greet(self.peer(a, b)))
            count = count + (1 if a == 0 else self.lat_ok(a).astype(jnp.int32))
        fold_count = jnp.int32(len(below_slots))
        for s in top_slots:
            fold_count = fold_count + (self.fold_peer(s) != self.lon).astype(jnp.int32)
        if self.turn is not None:

            @pl.when(self.top)
            def _():
                for s in top_slots:
                    q = self.fold_peer(s)

                    @pl.when(q != self.lon)
                    def _():
                        self.greet({"lat": self.lat, "lon": q})

                for s in below_slots:
                    self.greet({"lat": self.lat - 1, "lon": self.fold_peer(s)})

            @pl.when(self.below)
            def _():
                for s in below_slots:
                    self.greet({"lat": self.lat + 1, "lon": self.fold_peer(s)})

            count = count + jnp.where(self.top, fold_count, 0)
            count = count + jnp.where(self.below, len(below_slots), 0)
        return count

    def copy(self, src, dst, sems, to):
        return pltpu.make_async_remote_copy(
            src_ref=src,
            dst_ref=dst,
            send_sem=sems.at[0],
            recv_sem=sems.at[1],
            device_id=to,
            device_id_type=MESH,
        )

    def rim_copy(self, n, own, margins, centre, blocks, sems):
        a, b = self.SHIFTS[n]
        to = self.peer(a, b)
        if b:
            side = 1 if b == 1 else 0
            return self.copy(margins.at[side], blocks.at[2 - a, side], sems.at[:, n], to)
        src_rows, dst_rows = {
            1: ((0, 16), (8, 24)),
            2: ((8, 16), (0, 8)),
            -1: ((0, 16), (MARGIN + 16, MARGIN + 32)),
            -2: ((0, 8), (MARGIN + 32, MARGIN + 40)),
        }[a]
        return self.copy(
            own.at[:, src_rows[0] : src_rows[1]],
            centre.at[:, dst_rows[0] : dst_rows[1]],
            sems.at[:, n],
            to,
        )

    def fold_start(self, s, copy, src, dst, sem, same_lat):
        if not same_lat:
            copy().start()
            return
        own = self.fold_peer(s) == self.lon

        @pl.when(jnp.logical_not(own))
        def _():
            copy().start()

        @pl.when(own)
        def _():
            pltpu.make_async_copy(src, dst, sem).start()

    def fold_sent(self, s, copy, same_lat):
        if not same_lat:
            copy().wait_send()
            return

        @pl.when(self.fold_peer(s) != self.lon)
        def _():
            copy().wait_send()

    def fold_rim_ref(self, kind, s, src, dst):
        rows = (0, 16) if kind == 0 else (8, 16)
        to = {0: (0, 16), 1: (8, 16), 2: (16, 24)}[kind]
        lanes = slice(*{0: (128, 256), 3: (0, 128)}.get(s, (0, 256)))
        slot = s - (4 - dst.shape[0]) // 2
        return src.at[:, rows[0] : rows[1], lanes], dst.at[slot, :, to[0] : to[1], lanes]

    def fold_rim_copy(self, kind, s, src, dst, sems):
        a, b = self.fold_rim_ref(kind, s, src, dst)
        to = {"lat": self.lat + (0, -1, 1)[kind], "lon": self.fold_peer(s)}
        return self.copy(a, b, sems.at[:, 0 if kind == 0 else 1, s], to)

    def fold_rim_kinds(self, slots, kinds, body):
        @pl.when(self.top)
        def _():
            for s in slots:
                for kind in (0, 1):
                    if kind in kinds:
                        body(kind, s)

        @pl.when(self.below)
        def _():
            for s in slots:
                body(2, s)

    def fold_rim_start(self, slots, kinds, src, dst, sems):
        def body(kind, s):
            a, b = self.fold_rim_ref(kind, s, src, dst)
            self.fold_start(
                s,
                lambda: self.fold_rim_copy(kind, s, src, dst, sems),
                a,
                b,
                sems.at[1, 0, s],
                kind == 0,
            )

        self.fold_rim_kinds(slots, kinds, body)

    def fold_rim_finish(self, slots, kinds, src, dst, sems):
        @pl.when(self.top)
        def _():
            for s in slots:
                self.fold_rim_copy(0, s, src, dst, sems).wait_recv()
                self.fold_rim_copy(2, s, src, dst, sems).wait_recv()

        if 1 in kinds:

            @pl.when(self.below)
            def _():
                for s in slots:
                    self.fold_rim_copy(1, s, src, dst, sems).wait_recv()

        self.fold_rim_kinds(
            slots,
            kinds,
            lambda kind, s: self.fold_sent(
                s, lambda: self.fold_rim_copy(kind, s, src, dst, sems), kind == 0
            ),
        )


def first_exchange(
    lon_size, lat_size, turn, cells, edges, rim, bands, edges_in, fold_cells, fold_rim,
    edge_sem, band_sem, wet_sem, fold_sem, fold_wet_sem, fold_rim_sem
):
    links = Links(lon_size, lat_size, turn)
    count = links.meet([(1, 0), (-1, 0), (0, 1), (0, -1)], (1, 2), (1, 2))
    pl.semaphore_wait(links.barrier, count)

    def edge_copy(side):
        return links.copy(
            edges.at[side], edges_in.at[side], edge_sem.at[:, side], links.peer(0, 2 * side - 1)
        )

    def band_copies(side):
        first = ROWS - 3 if side == 0 else 0
        wet_from, wet_to = (ROWS - 1, 2) if side == 0 else (0, 0)
        to = links.peer(1 - 2 * side, 0)
        return (
            links.copy(
                cells.at[0:4, first : first + 3], bands.at[side, 0:4], band_sem.at[:, side], to
            ),
            links.copy(cells.at[4, wet_from], bands.at[side, 4, wet_to], wet_sem.at[:, side], to),
        )

    fold_parts = (
        lambda s: (cells.at[0:4, ROWS - 3 : ROWS], fold_cells.at[s - 1, 0:4], fold_sem.at[:, s - 1]),
        lambda s: (cells.at[4, ROWS - 1], fold_cells.at[s - 1, 4, 2], fold_wet_sem.at[:, s - 1]),
    )

    def fold_cell_copy(s, part):
        return links.copy(*part(s), {"lat": links.lat, "lon": links.fold_peer(s)})

    @pl.when(links.top)
    def _():
        for s in (1, 2):
            for part in fold_parts:
                a, b, sem = part(s)
                links.fold_start(
                    s, lambda s=s, part=part: fold_cell_copy(s, part), a, b, sem.at[1], True
                )

    for side in range(2):

        def send(side=side):
            for copy in band_copies(side):
                copy.start()

        links.when_lat(1 - 2 * side, send)
    for side in range(2):
        edge_copy(side).start()
    links.fold_rim_start((1, 2), (0, 2), rim, fold_rim, fold_rim_sem)

    for side in range(2):
        edge_copy(side).wait()
    for side in range(2):

        def arrived(side=side):
            for copy in band_copies(side):
                copy.wait_recv()

        def sent(side=side):
            for copy in band_copies(side):
                copy.wait_send()

        links.when_lat(2 * side - 1, arrived)
        links.when_lat(1 - 2 * side, sent)

    @pl.when(links.top)
    def _():
        for s in (1, 2):
            for part in fold_parts:
                fold_cell_copy(s, part).wait_recv()
                links.fold_sent(s, lambda s=s, part=part: fold_cell_copy(s, part), True)

    links.fold_rim_finish((1, 2), (0, 2), rim, fold_rim, fold_rim_sem)


def first_exchange_call(lon_size, lat_size, turn, collective_id):
    f32 = jnp.float32
    anywhere = pl.BlockSpec(memory_space=pl.ANY)
    dma = pltpu.SemaphoreType.DMA
    return pl.pallas_call(
        functools.partial(first_exchange, lon_size, lat_size, turn),
        out_shape=(
            jax.ShapeDtypeStruct((2, 5, 3, 2, LEVELS, LANES), f32),
            jax.ShapeDtypeStruct((2, 5, LEVELS, LANES), f32),
            jax.ShapeDtypeStruct((2, 5, 3, 2, LEVELS, LANES), f32),
            jax.ShapeDtypeStruct((2, 4, MARGIN, COLS), f32),
        ),
        in_specs=[anywhere] * 3,
        out_specs=(anywhere,) * 4,
        scratch_shapes=[dma((2, 2))] * 5 + [dma((2, 2, 4))],
        compiler_params=pltpu.CompilerParams(collective_id=collective_id, has_side_effects=True),
        name="first_exchange",
    )


def interior(
    lon_size, lat_size, seam_ref, cells_in, edges, rim_in, bands, edges_in, fold_cells, fold_rim, rim_own, margins,
    centre, blocks, moved, done, means, mean_margins,
    cells, halo, face_west, flux_north, part, sums, ghost, ghost_margins, cell_sem, rim_sem, ghost_sem
):
    f32 = jnp.float32
    links = Links(lon_size, lat_size)
    lat = links.lat
    count = links.meet(Links.SHIFTS)
    filled = pltpu.make_async_copy(cells_in, cells.at[:, 3 : 3 + ROWS], cell_sem.at[0])
    south = pltpu.make_async_copy(bands.at[0], cells.at[:, 0:3], cell_sem.at[1])
    north = pltpu.make_async_copy(bands.at[1], cells.at[:, ROWS + 3 : ROWS + 6], cell_sem.at[2])
    keep = pltpu.make_async_copy(
        rim_own, centre.at[:, MARGIN : MARGIN + ROWS], cell_sem.at[3]
    )
    fold_in = pltpu.make_async_copy(ghost, centre.at[:, MARGIN + ROWS : WIDE], cell_sem.at[4])
    filled.start()
    keep.start()
    links.when_lat(-1, south.start)
    links.when_lat(1, north.start)

    @pl.when(lat == 0)
    def _():
        cells[:, 0:3] = jnp.zeros((5, 3, 2, LEVELS, LANES), f32)

    level = lax.broadcasted_iota(jnp.int32, (LEVELS, LANES), 0)
    lane = lax.broadcasted_iota(jnp.int32, (LEVELS, LANES), 1)

    @pl.when(links.top)
    def _():
        turn_lanes, flip_rows, same_tile = turner(seam_ref)

        def image(tile):
            turned = [turn_lanes(tile(2 - n), tile(3 - n)) for n in range(3)]
            return [jnp.where(same_tile, turned[t], turned[t + 1]) for t in range(2)]

        def across(g, _):
            for f in range(4):
                for t, value in enumerate(image(lambda n: fold_cells[n // 2, f, 2 - g, n % 2])):
                    cells[f, ROWS + 3 + g, t] = -value if f < 2 else value
            return _

        lax.fori_loop(0, 3, across, 0)
        for t, value in enumerate(image(lambda n: fold_cells[n // 2, 4, 2, n % 2])):
            cells[4, ROWS + 3, t] = value

        def across_rim(f, _):
            sign = jnp.where(jnp.logical_or(f == SEA, f == TALLY), 1.0, -1.0)
            for q, first in enumerate((8, 0, 16)):

                def tile(n):
                    lanes = slice((n % 2) * LANES, (n % 2 + 1) * LANES)
                    return fold_rim[n // 2, f, first : first + 8, lanes]

                for t, value in enumerate(image(tile)):
                    ghost[f, 8 * q : 8 * q + 8, t * LANES : (t + 1) * LANES] = flip_rows(value) * sign
            return _

        lax.fori_loop(0, 4, across_rim, 0)
        fold_in.start()
        for block in range(2):
            for pair in range(2):
                tiles = []
                for g in range(4):
                    first = 8 * (g % 2) if block == 0 else 16
                    rows = slice(first, first + 8)
                    f = 2 * pair + g // 2
                    tiles.append((ghost[f, rows, 0:LANES], ghost[f, rows, LANES:COLS]))
                packed = pack_margins(tiles)
                for side in range(2):
                    ghost_margins[block, side, pair] = packed[side]

    def ghost_copies(row):
        for side in range(2):
            to = links.peer(-row, 2 * side - 1)
            if row == 0:
                yield links.copy(
                    ghost_margins.at[:, side], blocks.at[3:5, side], ghost_sem.at[:, side], to
                )
            else:
                yield links.copy(
                    ghost_margins.at[0, side], blocks.at[4, side], ghost_sem.at[:, 2 + side], to
                )
        if row:
            yield links.copy(
                ghost.at[:, 0:8],
                centre.at[:, MARGIN + 32 : WIDE],
                ghost_sem.at[:, 4],
                links.peer(-1, 0),
            )

    def back(x, n):
        return pltpu.roll(x, LANES - n, 1)

    packed = []
    for f in range(5):
        west = edges_in[1, f]
        own = edges[0, f]
        packed.append((west, own))
    speed = 0.5 * (back(packed[0][0], 2) + packed[0][1]) * back(packed[4][0], 2) * packed[4][1]
    face_west[4] = speed
    for f in range(4):
        west, own = packed[f]
        inner = back(west, 2)
        ew = back(west, 1) - west
        eo = back(own, 1) - own
        face_west[f] = weno_flux(
            ew,
            back(ew, 1),
            own - inner,
            eo,
            back(eo, 1),
            inner,
            own,
            COURANT * speed,
            (COURANT / 6.0) * jnp.abs(speed),
            speed >= 0.0,
        )

    filled.wait()

    def north_face(face):
        speeds = []
        for t in range(2):
            speed = (
                0.5
                * (cells[1, face + 2, t] + cells[1, face + 3, t])
                * cells[4, face + 2, t]
                * cells[4, face + 3, t]
            )
            flux_north[4, face, t] = speed
            speeds.append(
                (COURANT * speed, (COURANT / 6.0) * jnp.abs(speed), speed >= 0.0)
            )
        for f in range(4):
            for t in range(2):
                q = [cells[f, face + n, t] for n in range(6)]
                e = [q[n + 1] - q[n] for n in range(5)]
                flux_north[f, face, t] = weno_flux(*e, q[2], q[3], *speeds[t])

    def north_loop(face, _):
        north_face(face)
        return _

    lax.fori_loop(3, 14, north_loop, 0)

    def rim_copy(n):
        return links.rim_copy(n, rim_own, margins, centre, blocks, rim_sem)

    pl.semaphore_wait(links.barrier, count)
    for n, (a, b) in enumerate(Links.SHIFTS):
        links.when_lat(a, lambda n=n: rim_copy(n).start())

    @pl.when(links.top)
    def _():
        for row in range(2):
            for copy in ghost_copies(row):
                copy.start()

    first_lane = lane == 0
    last_lane = lane == LANES - 1

    def unpack(r, _):
        for f in range(5):
            east = pltpu.roll(edges_in[0, f], LANES - 3 * r, 1)
            west = pltpu.roll(edges_in[1, f], LANES - 3 - 3 * r, 1)
            halo[f, r] = jnp.where(lane < LANES // 2, east, west)
        return _

    lax.fori_loop(0, ROWS, unpack, 0)

    def ahead_1(x):
        turned = [pltpu.roll(v, LANES - 1, 1) for v in x]
        return [jnp.where(last_lane, turned[(n + 1) % 3], turned[n]) for n in range(3)]

    def ahead_2(x):
        turned = [pltpu.roll(v, LANES - 2, 1) for v in x]
        return [
            jnp.where(lane >= LANES - 2, turned[(n + 1) % 3], turned[n]) for n in range(2)
        ]

    def behind_1(x):
        turned = [pltpu.roll(v, 1, 1) for v in x]
        return [jnp.where(first_lane, turned[(n + 2) % 3], turned[n]) for n in range(2)]

    def behind_2(x):
        turned = [pltpu.roll(v, 2, 1) for v in x]
        return [jnp.where(lane < 2, turned[(n + 2) % 3], turned[n]) for n in range(2)]

    def east_loop(r, _):
        wet = [cells[4, r + 3, 0], cells[4, r + 3, 1], halo[4, r]]
        wet_next = ahead_1(wet)
        gaps, nexts, firsts = [], [], []
        for f in range(4):
            q = [cells[f, r + 3, 0], cells[f, r + 3, 1], halo[f, r]]
            nxt = ahead_1(q)
            firsts.append(q)
            nexts.append(nxt)
            gaps.append([nxt[n] - q[n] for n in range(3)])
        speeds = []
        for t in range(2):
            speed = 0.5 * (firsts[0][t] + nexts[0][t]) * wet[t] * wet_next[t]
            speeds.append(speed)
        behind = []

        def difference(x, first):
            turned = [pltpu.roll(v, 1, 1) for v in x]
            return (
                x[0] - jnp.where(first_lane, first, turned[0]),
                x[1] - jnp.where(first_lane, turned[0], turned[1]),
            )

        def west_of(f):
            return pltpu.roll(face_west[f], LANES - 3 * r, 1)

        spread = difference(speeds, west_of(4))
        for t in range(2):
            part[4, r, t] = spread[t]
        for f in range(4):
            e = gaps[f]
            em1 = behind_1(e)
            em2 = behind_2(e)
            ep1 = ahead_1(e)
            ep2 = ahead_2(e)
            behind.append(em1)
            flux = [
                weno_flux(
                    em2[t],
                    em1[t],
                    e[t],
                    ep1[t],
                    ep2[t],
                    firsts[f][t],
                    nexts[f][t],
                    COURANT * speeds[t],
                    (COURANT / 6.0) * jnp.abs(speeds[t]),
                    speeds[t] >= 0.0,
                )
                for t in range(2)
            ]
            lost = difference(flux, west_of(f))
            for t in range(2):
                part[f, r, t] = lost[t]
        for t in range(2):
            part[5, r, t] = 0.8 * (gaps[3][t] + behind[3][t]) - 0.2 * (
                gaps[2][t] + behind[2][t]
            )
        return _

    lax.fori_loop(0, ROWS, east_loop, 0)

    links.when_lat(-1, south.wait)
    links.when_lat(1, north.wait)

    def outer_loop(n, _):
        north_face(n)
        north_face(n + 14)
        return _

    lax.fori_loop(0, 3, outer_loop, 0)

    def down_sum(x):
        for s in (1, 2, 4):
            x = x + jnp.where(level >= s, pltpu.roll(x, s, 0), 0.0)
        return x

    def up_sum(x):
        for s in (1, 2, 4):
            x = x + jnp.where(level < LEVELS - s, pltpu.roll(x, LEVELS - s, 0), 0.0)
        return x

    total_rows = ROWS * lat_size

    def combine(r, _):
        row = (lat * ROWS + r).astype(f32)
        coriolis = CORIOLIS * (2.0 * (row + 0.5) / total_rows - 1.0)
        for t in range(2):
            q = [cells[f, r + 3, t] for f in range(4)]
            wet = cells[4, r + 3, t]
            spread = part[4, r, t] + (flux_north[4, r + 1, t] - flux_north[4, r, t])
            lift = jnp.where(level >= 1, (-0.5 * COURANT) * up_sum(spread), 0.0)
            rates = []
            for f in range(4):
                vertical = lift * (pltpu.roll(q[f], 1, 0) + q[f])
                rates.append(
                    (pltpu.roll(vertical, LEVELS - 1, 0) - vertical)
                    - part[f, r, t]
                    - (flux_north[f, r + 1, t] - flux_north[f, r, t])
                )
            slope_east = part[5, r, t]
            slope_north = 0.8 * (cells[3, r + 4, t] - cells[3, r + 2, t]) - 0.2 * (
                cells[2, r + 4, t] - cells[2, r + 2, t]
            )
            grad_east = 0.5 * (down_sum(slope_east) - 0.5 * slope_east)
            grad_north = 0.5 * (down_sum(slope_north) - 0.5 * slope_north)
            force_zonal = rates[0] + coriolis * q[1] - PRESSURE_GAIN * grad_east
            force_merid = rates[1] - coriolis * q[0] - PRESSURE_GAIN * grad_north
            sums[0, t, pl.ds(r, 1), :] = jnp.sum(wet * force_zonal, axis=0, keepdims=True)
            sums[1, t, pl.ds(r, 1), :] = jnp.sum(wet * force_merid, axis=0, keepdims=True)
            moved[0, r, t] = q[0] + force_zonal
            moved[1, r, t] = q[1] + force_merid
            done[0, t, pl.ds(r, LEVELS, stride=ROWS), :] = wet * (q[2] + rates[2])
            done[1, t, pl.ds(r, LEVELS, stride=ROWS), :] = wet * (q[3] + rates[3])
        return _

    lax.fori_loop(0, ROWS, combine, 0)

    for t in range(2):
        lanes = slice(t * LANES, (t + 1) * LANES)
        column = jnp.maximum(rim_in[TALLY, :, lanes], 1.0)
        for f in range(2):
            sums[f, t] = sums[f, t] / column
            means[f, :, lanes] = sums[f, t]
    tiles = []
    for g in range(4):
        rows = slice(8 * (g % 2), 8 * (g % 2) + 8)
        tiles.append((sums[g // 2, 0, rows, :], sums[g // 2, 1, rows, :]))
    mean_margins[0, 0], mean_margins[1, 0] = pack_margins(tiles)

    keep.wait()
    for n, (a, b) in enumerate(Links.SHIFTS):
        links.when_lat(-a, lambda n=n: rim_copy(n).wait_recv())
    for n, (a, b) in enumerate(Links.SHIFTS):
        links.when_lat(a, lambda n=n: rim_copy(n).wait_send())

    @pl.when(links.top)
    def _():
        fold_in.wait()
        for copy in ghost_copies(0):
            copy.wait_recv()
        for row in range(2):
            for copy in ghost_copies(row):
                copy.wait_send()

    @pl.when(links.below)
    def _():
        for copy in ghost_copies(1):
            copy.wait_recv()


def interior_call(lon_size, lat_size, collective_id):
    f32 = jnp.float32
    vmem = pl.BlockSpec(memory_space=pltpu.VMEM)
    anywhere = pl.BlockSpec(memory_space=pl.ANY)
    dma = pltpu.SemaphoreType.DMA
    return pl.pallas_call(
        functools.partial(interior, lon_size, lat_size),
        out_shape=(
            jax.ShapeDtypeStruct((4, WIDE, COLS), f32),
            jax.ShapeDtypeStruct((5, 2, 2, LEVELS, LANES), f32),
            jax.ShapeDtypeStruct((2, ROWS, 2, LEVELS, LANES), f32),
            jax.ShapeDtypeStruct((2, 2, LEVELS * ROWS, LANES), f32),
            jax.ShapeDtypeStruct((2, ROWS, COLS), f32),
            jax.ShapeDtypeStruct((2, 1, LEVELS, LANES), f32),
        ),
        in_specs=[pl.BlockSpec(memory_space=pltpu.SMEM)]
        + [anywhere, vmem, vmem, anywhere, vmem, vmem, vmem, anywhere, anywhere],
        out_specs=(anywhere, anywhere, vmem, vmem, vmem, vmem),
        scratch_shapes=[
            pltpu.VMEM((5, ROWS + 6, 2, LEVELS, LANES), f32),
            pltpu.VMEM((5, ROWS, LEVELS, LANES), f32),
            pltpu.VMEM((5, LEVELS, LANES), f32),
            pltpu.VMEM((5, ROWS + 1, 2, LEVELS, LANES), f32),
            pltpu.VMEM((6, ROWS, 2, LEVELS, LANES), f32),
            pltpu.VMEM((2, 2, ROWS, LANES), f32),
            pltpu.VMEM((4, MARGIN, COLS), f32),
            pltpu.VMEM((2, 2, 2, LEVELS, LANES), f32),
            dma((5,)),
            dma((2, 14)),
            dma((2, 5)),
        ],
        compiler_params=pltpu.CompilerParams(collective_id=collective_id, has_side_effects=True),
        name="interior",
    )


def second_exchange(
    lon_size, lat_size, turn, means, margins, centre, blocks, fold_rim, rim_sem, fold_rim_sem
):
    links = Links(lon_size, lat_size, turn)
    count = links.meet(Links.SHIFTS, (0, 1, 2, 3), (0, 1, 2, 3))
    pl.semaphore_wait(links.barrier, count)
    slots, kinds = (0, 1, 2, 3), (0, 1, 2)

    def rim_copy(n):
        return links.rim_copy(n, means, margins, centre, blocks, rim_sem)

    links.fold_rim_start(slots, kinds, means, fold_rim, fold_rim_sem)
    for n, (a, b) in enumerate(Links.SHIFTS):
        links.when_lat(a, lambda n=n: rim_copy(n).start())
    for n, (a, b) in enumerate(Links.SHIFTS):
        links.when_lat(-a, lambda n=n: rim_copy(n).wait_recv())
    links.fold_rim_finish(slots, kinds, means, fold_rim, fold_rim_sem)
    for n, (a, b) in enumerate(Links.SHIFTS):
        links.when_lat(a, lambda n=n: rim_copy(n).wait_send())


def second_exchange_call(lon_size, lat_size, turn, collective_id):
    f32 = jnp.float32
    anywhere = pl.BlockSpec(memory_space=pl.ANY)
    dma = pltpu.SemaphoreType.DMA
    return pl.pallas_call(
        functools.partial(second_exchange, lon_size, lat_size, turn),
        out_shape=(
            jax.ShapeDtypeStruct((2, WIDE, COLS), f32),
            jax.ShapeDtypeStruct((5, 2, 1, LEVELS, LANES), f32),
            jax.ShapeDtypeStruct((4, 2, MARGIN, COLS), f32),
        ),
        in_specs=[anywhere] * 2,
        out_specs=(anywhere,) * 3,
        scratch_shapes=[dma((2, 14)), dma((2, 2, 4))],
        compiler_params=pltpu.CompilerParams(collective_id=collective_id, has_side_effects=True),
        name="second_exchange",
    )


def finish(
    lat_size, seam_ref, centre_a, blocks_a, centre_b, blocks_b, fold_b, means, rim_own, moved, done_in,
    u_out, v_out, t_out, s_out, sea_out, zon_out, mer_out,
    wave, done, flat, tally, sems
):
    f32 = jnp.float32
    lat = lax.axis_index("lat")
    total_rows = ROWS * lat_size
    width = COLS + LANES
    stores = []
    for f, ref in ((2, t_out), (3, s_out)):
        for t in range(2):
            lanes = slice(t * LANES, (t + 1) * LANES)
            stores.append(pltpu.make_async_copy(done_in.at[f - 2, t], ref.at[:, lanes], sems.at[2 * f + t]))
    for copy in stores:
        copy.start()

    lane = lax.broadcasted_iota(jnp.int32, (LEVELS, LANES), 1)
    own_rows = slice(MARGIN, MARGIN + ROWS)
    row = lax.broadcasted_iota(jnp.int32, (WIDE, width), 0) + (lat * ROWS - MARGIN)
    sources = ((0, 1), (1, 0), (1, 1), (2, 0), (2, 1), (3, 0), (3, 1), (4, 0))
    for f in range(6):
        centre, blocks, n = (centre_a, blocks_a, f) if f < 4 else (centre_b, blocks_b, f - 4)
        wave[f, :, 0:COLS] = centre[n]
        for i, (block, part) in enumerate(sources):
            lead = MARGIN * (2 * (n % 2) + part)
            from_east = blocks[block, 0, n // 2]
            if lead:
                from_east = pltpu.roll(from_east, LANES - lead, 1)
            from_west = pltpu.roll(blocks[block, 1, n // 2], LANES - MARGIN - lead, 1)
            wave[f, 8 * i : 8 * i + 8, COLS:width] = jnp.where(
                lane < LANES // 2, from_east, from_west
            )
    for f in range(2):
        wave[MEANZ + f, own_rows, 0:COLS] = means[f]
    for n, empty in ((0, MARGIN), (1, 8)):

        @pl.when(lat == n)
        def _():
            wave[0:6, 0:empty] = jnp.zeros((6, empty, width), f32)

    def unfold(ghost_tiles):
        turn_lanes, flip_rows, same_tile = turner(seam_ref)

        def mean(n, _):
            for to, source in ghost_tiles:

                def tile(m):
                    at = slice((m % 2) * LANES, (m % 2 + 1) * LANES)
                    return fold_b[m // 2, n, source : source + 8, at]

                turned = {m: turn_lanes(tile(m + 4), tile(m + 5)) for m in range(-3, 2)}
                image = {
                    m: -flip_rows(jnp.where(same_tile, turned[m], turned[m - 1]))
                    for m in range(-2, 2)
                }
                f = n + MEANZ
                wave[f, to : to + 8, 0:128] = image[0]
                wave[f, to : to + 8, 128:256] = image[-1]
                wave[f, to : to + 8, 256:384] = jnp.where(lane < LANES // 2, image[-2], image[1])
            return _

        lax.fori_loop(0, 2, mean, 0)

    pl.when(lat == lat_size - 1)(lambda: unfold(((40, 8), (48, 0), (56, 16))))
    pl.when(lat == lat_size - 2)(lambda: unfold(((56, 8),)))

    mirrored = jnp.minimum(row, 2 * total_rows - 1 - row).astype(f32)
    wide_tally = wave[TALLY]
    wave[6] = jnp.where(wide_tally > 0.0, 1.0, 0.0)
    wave[TALLY] = wide_tally * (0.5 * WAVE_MASS / LEVELS)
    wave[7] = (CORIOLIS / SUBSTEPS) * (2.0 * (mirrored + 0.5) / total_rows - 1.0)
    wave[MEANZ] = wave[MEANZ] * (1.0 / SUBSTEPS)
    wave[MEANM] = wave[MEANM] * (1.0 / SUBSTEPS)

    def east_difference(x):
        return pltpu.roll(x, width - 1, 1) - pltpu.roll(x, 1, 1)

    def north_difference(x):
        return pltpu.roll(x, WIDE - 1, 0) - pltpu.roll(x, 1, 0)

    def substep(n, _):
        thick = wave[TALLY]
        wet = wave[6]
        zonal = wave[ZON]
        merid = wave[MER]
        level_next = wet * (
            wave[SEA] - (east_difference(thick * zonal) + north_difference(thick * merid))
        )
        turn_rate = wave[7]
        wave[SEA] = level_next
        wave[ZON] = wet * (
            zonal
            - (0.5 * WAVE_MOMENTUM) * east_difference(level_next)
            + (turn_rate * merid + wave[MEANZ])
        )
        wave[MER] = wet * (
            merid
            - (0.5 * WAVE_MOMENTUM) * north_difference(level_next)
            + (wave[MEANM] - turn_rate * zonal)
        )
        return _

    lax.fori_loop(0, SUBSTEPS, substep, 0)

    for f, ref in enumerate((sea_out, zon_out, mer_out)):
        copy = pltpu.make_async_copy(wave.at[f, own_rows, 0:COLS], ref, sems.at[8 + f])
        copy.start()
        stores.append(copy)
    for t in range(2):
        lanes = slice(t * LANES, (t + 1) * LANES)
        tally[t] = rim_own[TALLY, :, lanes]
        for f in range(2):
            flat[f, t] = wave[ZON + f, own_rows, lanes] - rim_own[ZON + f, :, lanes] - means[f, :, lanes]
    level = lax.broadcasted_iota(jnp.int32, (LEVELS, LANES), 0).astype(f32)

    def last(r, _):
        for t in range(2):
            wet = level < tally[t, pl.ds(r, 1), :]
            for f in range(2):
                shift = flat[f, t, pl.ds(r, 1), :]
                done[f, t, pl.ds(r, LEVELS, stride=ROWS), :] = jnp.where(
                    wet, moved[f, r, t] + shift, 0.0
                )
        return _

    lax.fori_loop(0, ROWS, last, 0)

    for f, ref in ((0, u_out), (1, v_out)):
        for t in range(2):
            lanes = slice(t * LANES, (t + 1) * LANES)
            copy = pltpu.make_async_copy(done.at[f, t], ref.at[:, lanes], sems.at[2 * f + t])
            copy.start()
            stores.append(copy)
    for copy in stores:
        copy.wait()


def finish_call(lat_size, *arguments):
    f32 = jnp.float32
    deep = jax.ShapeDtypeStruct((LEVELS * ROWS, COLS), f32)
    flat = jax.ShapeDtypeStruct((ROWS, COLS), f32)
    vmem = pl.BlockSpec(memory_space=pltpu.VMEM)
    anywhere = pl.BlockSpec(memory_space=pl.ANY)
    return pl.pallas_call(
        functools.partial(finish, lat_size),
        out_shape=(deep,) * 4 + (flat,) * 3,
        in_specs=[pl.BlockSpec(memory_space=pltpu.SMEM)] + [vmem] * 9,
        out_specs=(anywhere,) * 7,
        scratch_shapes=[
            pltpu.VMEM((8, WIDE, COLS + LANES), f32),
            pltpu.VMEM((2, 2, LEVELS * ROWS, LANES), f32),
            pltpu.VMEM((2, 2, ROWS, LANES), f32),
            pltpu.VMEM((2, ROWS, LANES), f32),
            pltpu.SemaphoreType.DMA((11,)),
        ],
        name="finish",
    )(*arguments)


def on_device(lon_size, lat_size, *arguments):
    *fields, sea, zon, mer, tally, seam = arguments
    deep = [x.reshape(LEVELS * ROWS, COLS) for x in fields]
    turn = lax.rem(lax.shift_right_logical(seam[0], 8) + lax.axis_index("lon"), lon_size)
    cells, edges, rim_own, margins = prepare_call(*deep, sea, zon, mer, tally)
    bands, edges_in, fold_cells, fold_a = lax.switch(
        turn,
        [first_exchange_call(lon_size, lat_size, n, n) for n in range(lon_size)],
        cells,
        edges,
        rim_own,
    )
    centre_a, blocks_a, moved, done, means, mean_margins = interior_call(
        lon_size, lat_size, 2 * lon_size
    )(seam, cells, edges, rim_own, bands, edges_in, fold_cells, fold_a, rim_own, margins)
    centre_b, blocks_b, fold_b = lax.switch(
        turn,
        [second_exchange_call(lon_size, lat_size, n, lon_size + n) for n in range(lon_size)],
        means,
        mean_margins,
    )
    out = finish_call(
        lat_size, seam, centre_a, blocks_a, centre_b, blocks_b, fold_b, means, rim_own, moved, done
    )
    return tuple(x.reshape(LEVELS, ROWS, COLS) for x in out[:4]) + tuple(out[4:])


def solution(mesh):
    deep = P(None, "lat", "lon")
    flat = P("lat", "lon")
    return jax.shard_map(
        functools.partial(on_device, mesh.shape["lon"], mesh.shape["lat"]),
        mesh=mesh,
        in_specs=(deep,) * 4 + (flat,) * 4 + (P("lon"),),
        out_specs=(deep,) * 4 + (flat,) * 3,
        check_vma=False,
    )
```

profile of v0, /device:TPU:7, one launch (start us, length us, event | category | flops | bytes accessed | tf_op | source)
XLA Modules:
  0.0 50.6 jit_solution(14360378265989384002)
XLA Ops:
  0.6 0.0 copy-start
  0.6 0.7 %copy-done = s32[256]{0:T(256)S(1)} copy-done((s32[256]{0:T(256)S(1)}, s32[256]{0:T(256)}, u32[]{:S(2)}) %copy-start) | copy-done | bytes 1048
  1.3 0.5 %slice.3 = s32[1]{0:T(128)} slice(s32[256]{0:T(256)S(1)} %copy-done), slice={[0:1]} | slice | bytes 8 | tf_op jit(solution)/shard_map/slice | solution.py:1012
  2.5 3.3 %prepare.1 = (f32[5,16,2,8,128]{4,3,2,1,0:T(8,128)S(1)}, f32[2,5,8,128]{3,2,1,0:T(8,128)S(1)}, f32[4,16,256]{2,1,0:T(8,128)S(1)}, f32[2,2,8,128]{3,2,1,0:T(8,128)}) custom-call(f32[128,256]{1,0:T(8,128)} %bitcast.9, f32[128,256]{1,0:T(8,128)} %bitcast.10, f32[128,256]{1,0:T(8,128)} %bitcast.11, f32[128,256]{1,0:T(8,128)} %bitcast.12, f32[16,256]{1,0:T(8,128)} %sea_in.1, ...), custom_call_target="tpu_custom_call" | custom-call | tf_op jit(solution)/shard_map/prepare/pallas_call | solution.py:142
  5.8 13.7 %conditional.2 = ((f32[2,5,3,2,8,128]{5,4,3,2,1,0:T(8,128)S(1)}, f32[2,5,8,128]{3,2,1,0:T(8,128)S(1)}, f32[2,5,3,2,8,128]{5,4,3,2,1,0:T(8,128)S(1)}, f32[2,4,24,256]{3,2,1,0:T(8,128)S(1)})) conditional(s32[]{:T(128)} %clamp.4, (f32[5,16,2,8,128]{4,3,2,1,0:T(8,128)S(1)}, f32[2,5,8,128]{3,2,1,0:T(8,128)S(1)}, ...), branch_computations={%region_0.0_spmd, %region_1.0_spmd, %region_2.0_spmd, %region_3.0_... | conditional | bytes 8 | solution.py:1014
  5.8 13.6 %first_exchange.21 = (f32[2,5,3,2,8,128]{5,4,3,2,1,0:T(8,128)S(1)}, f32[2,5,8,128]{3,2,1,0:T(8,128)S(1)}, f32[2,5,3,2,8,128]{5,4,3,2,1,0:T(8,128)S(1)}, f32[2,4,24,256]{3,2,1,0:T(8,128)S(1)}) custom-call(f32[5,16,2,8,128]{4,3,2,1,0:T(8,128)S(1)} %get-tuple-element.175.cells, f32[2,5,8,128]{3,2,1,0:T(8,128)S(1)} %get-tuple-element.176.edges, ...), custom_call_target="tpu_custom_call" | custom-call | tf_op jit(solution)/shard_map/cond/branch_5_fun/first_exchange/pallas_call | solution.py:1014
  19.5 17.2 %interior.1 = (f32[4,64,256]{2,1,0:T(8,128)}, f32[5,2,2,8,128]{4,3,2,1,0:T(8,128)}, f32[2,16,2,8,128]{4,3,2,1,0:T(8,128)}, f32[2,2,128,128]{3,2,1,0:T(8,128)}, f...) custom-call(s32[256]{0:T(256)} %seam_ref.3, f32[5,16,2,8,128]{4,3,2,1,0:T(8,128)S(1)} %get-tuple-element.271.cells_in, ...), custom_call_target="tpu_custom_call" | custom-call | tf_op jit(solution)/shard_map/interior/pallas_call | solution.py:1021
  36.6 8.1 %conditional.3 = ((f32[2,64,256]{2,1,0:T(8,128)S(1)}, f32[5,2,1,8,128]{4,3,2,1,0:T(8,128)S(1)}, f32[4,2,24,256]{3,2,1,0:T(8,128)S(1)})) conditional(s32[]{:T(128)} %clamp.4, (f32[2,16,256]{2,1,0:T(8,128)S(1)}, f32[2,1,8,128]{3,2,1,0:T(8,128)S(1)}) %tuple.105, (f32[2,16,256]{2,1,0:T(8,128)S(1)}, ...), branch_computations={%region_16.0_spmd, %region_17.0_spmd, %region_18.0_spmd, %region_1... | conditional | bytes 8 | solution.py:1024
  36.9 7.7 %second_exchange.21 = (f32[2,64,256]{2,1,0:T(8,128)S(1)}, f32[5,2,1,8,128]{4,3,2,1,0:T(8,128)S(1)}, f32[4,2,24,256]{3,2,1,0:T(8,128)S(1)}) custom-call(f32[2,16,256]{2,1,0:T(8,128)S(1)} %get-tuple-element.218.means, f32[2,1,8,128]{3,2,1,0:T(8,128)S(1)} %get-tuple-element.219.margins), custom_call_target="tpu_custom_call" | custom-call | tf_op jit(solution)/shard_map/cond/branch_5_fun/second_exchange/pallas_call | solution.py:1024
  44.8 5.6 %finish.1 = (f32[128,256]{1,0:T(8,128)}, f32[128,256]{1,0:T(8,128)}, f32[128,256]{1,0:T(8,128)}, f32[128,256]{1,0:T(8,128)}, f32[16,256]{1,0:T(8,128)}, /*index=5*/f32[16,256]{1,0:T(8,128)}, f32[16,256]{1,0:T(8,128)}) custom-call(s32[256]{0:T(256)} %seam_ref.3, f32[4,64,256]{2,1,0:T(8,128)} %get-tuple-element.279.centre_a, ...), custom_call_target="tpu_custom_call" | custom-call | tf_op jit(solution)/shard_map/finish/pallas_call | solution.py:993
Async XLA Ops:
  0.6 0.7 %copy-start = (s32[256]{0:T(256)S(1)}, s32[256]{0:T(256)}, u32[]{:S(2)}) copy-start(s32[256]{0:T(256)} %seam_ref.3) | copy-start | bytes 3076
where the time goes:
time: 50.9 us; the launch traced here: 50.6 us
  Pallas kernels  47.3 us (93%)
  between operations  1.52 us (3%)
  local copies, waits for them, and re-layouts  1.19 us (2%)
  loops' own time  0.52 us (1%)
    pallas_call x1, Pallas kernels, on_device(): interior_call(lon_size, lat_size, 2 * lon_size)  17.2 us
    pallas_call x1, Pallas kernels, on_device(): lax.switch(turn, [first_exchange_call(lon_size, lat_size, n, n) for n in...  13.6 us
    pallas_call x1, Pallas kernels, on_device(): lax.switch(turn, [second_exchange_call(lon_size, lat_size, n, lon_size +...  7.67 us
    pallas_call x1, Pallas kernels, finish_call(): pl.pallas_call(functools.partial(finish, lat_size), out_shape=(deep,) * 4...  5.6 us
    pallas_call x1, Pallas kernels, prepare_call(): pl.pallas_call(prepare, out_shape=(jax.ShapeDtypeStruct((5, ROWS, 2, LEVE...  3.26 us

commit v1 on v0

--- a/solution.py
+++ b/solution.py
@@ -47,10 +47,10 @@
     return lax.rem(value + 2 * size, size)
 
 
-def turner(seam_ref):
+def turner(fold_ref):
     lane = lax.broadcasted_iota(jnp.int32, (LEVELS, LANES), 1)
     level = lax.broadcasted_iota(jnp.int32, (LEVELS, LANES), 0)
-    first_partner = jnp.full((LEVELS, LANES), seam_ref[0], jnp.int32)
+    first_partner = jnp.full((LEVELS, LANES), fold_ref[1], jnp.int32)
     upper = jnp.bitwise_and(first_partner, LANES) != 0
     base = jnp.bitwise_and(first_partner, LANES - 1)
     picked = jnp.bitwise_and(base - lane, LANES - 1)
@@ -81,11 +81,14 @@
 
 
 def prepare(
-    u_in, v_in, t_in, s_in, sea_in, zon_in, mer_in, tally_in, cells, edges, rim, margins,
-    raw, tally_raw, flat, sems
+    lon_size, u_in, v_in, t_in, s_in, sea_in, zon_in, mer_in, tally_in, seam_in, cells, edges, rim, margins, fold,
+    raw, tally_raw, flat, seam, sems
 ):
     f32 = jnp.float32
-    loads = [pltpu.make_async_copy(tally_in, tally_raw, sems.at[11])]
+    loads = [
+        pltpu.make_async_copy(seam_in, seam, sems.at[12]),
+        pltpu.make_async_copy(tally_in, tally_raw, sems.at[11]),
+    ]
     for f, ref in enumerate((u_in, v_in, t_in, s_in)):
         for t in range(2):
             lanes = slice(t * LANES, (t + 1) * LANES)
@@ -96,6 +99,8 @@
         copy.start()
     for copy in loads:
         copy.wait()
+    fold[0] = lax.rem(lax.shift_right_logical(seam[0], 8) + lax.axis_index("lon"), lon_size)
+    fold[1] = seam[0]
     level = lax.broadcasted_iota(jnp.int32, (LEVELS, LANES), 0).astype(f32)
     lane = lax.broadcasted_iota(jnp.int32, (LEVELS, LANES), 1)
     for t in range(2):
@@ -132,28 +137,30 @@
             edges[1, f] = jnp.where(mine, pltpu.roll(tiles[1], 3 * r + 3, 1), edges[1, f])
         return _
 
-    lax.fori_loop(0, ROWS, arrange, 0)
-
-
-def prepare_call(*arguments):
+    lax.fori_loop(0, ROWS, arrange, 0, unroll=16)
+
+
+def prepare_call(lon_size, *arguments):
     f32 = jnp.float32
     vmem = pl.BlockSpec(memory_space=pltpu.VMEM)
     anywhere = pl.BlockSpec(memory_space=pl.ANY)
     return pl.pallas_call(
-        prepare,
+        functools.partial(prepare, lon_size),
         out_shape=(
             jax.ShapeDtypeStruct((5, ROWS, 2, LEVELS, LANES), f32),
             jax.ShapeDtypeStruct((2, 5, LEVELS, LANES), f32),
             jax.ShapeDtypeStruct((4, ROWS, COLS), f32),
             jax.ShapeDtypeStruct((2, 2, LEVELS, LANES), f32),
+            jax.ShapeDtypeStruct((2,), jnp.int32),
         ),
-        in_specs=[anywhere] * 8,
-        out_specs=(vmem,) * 4,
+        in_specs=[anywhere] * 9,
+        out_specs=(vmem,) * 4 + (pl.BlockSpec(memory_space=pltpu.SMEM),),
         scratch_shapes=[
             pltpu.VMEM((4, 2, LEVELS * ROWS, LANES), f32),
             pltpu.VMEM((ROWS, COLS), jnp.int32),
             pltpu.VMEM((2, ROWS, LANES), f32),
-            pltpu.SemaphoreType.DMA((12,)),
+            pltpu.SMEM((COLS,), jnp.int32),
+            pltpu.SemaphoreType.DMA((13,)),
         ],
         name="prepare",
     )(*arguments)
@@ -161,6 +168,8 @@
 
 class Links:
     SHIFTS = [(a, b) for a in (1, -1, 2, -2, 0) for b in (0, 1, -1) if (a, b) != (0, 0)]
+    NEAR = [n for n, (a, b) in enumerate(SHIFTS) if abs(a) < 2]
+    FAR = [n for n, (a, b) in enumerate(SHIFTS) if abs(a) == 2]
 
     def __init__(self, lon_size, lat_size, turn=None):
         self.lon = lax.axis_index("lon")
@@ -248,6 +257,16 @@
             to,
         )
 
+    def far_copy(self, n, own, margins, rows, blocks, sems):
+        a, b = self.SHIFTS[n]
+        to = self.peer(a, b)
+        side = 0 if a > 0 else 1
+        if b:
+            edge = 1 if b == 1 else 0
+            return self.copy(margins.at[edge], blocks.at[side, edge], sems.at[:, n], to)
+        src = slice(8, 16) if a > 0 else slice(0, 8)
+        return self.copy(own.at[:, src], rows.at[side], sems.at[:, n], to)
+
     def fold_start(self, s, copy, src, dst, sem, same_lat):
         if not same_lat:
             copy().start()
@@ -334,11 +353,12 @@
 
 
 def first_exchange(
-    lon_size, lat_size, turn, cells, edges, rim, bands, edges_in, fold_cells, fold_rim,
-    edge_sem, band_sem, wet_sem, fold_sem, fold_wet_sem, fold_rim_sem
+    lon_size, lat_size, turn, cells, edges, rim, margins, bands, edges_in, fold_cells, fold_rim, far_rows, far_blocks,
+    far_sem, edge_sem, band_sem, wet_sem, fold_sem, fold_wet_sem, fold_rim_sem
 ):
     links = Links(lon_size, lat_size, turn)
-    count = links.meet([(1, 0), (-1, 0), (0, 1), (0, -1)], (1, 2), (1, 2))
+    far = [Links.SHIFTS[n] for n in Links.FAR]
+    count = links.meet([(1, 0), (-1, 0), (0, 1), (0, -1)] + far, (1, 2), (1, 2))
     pl.semaphore_wait(links.barrier, count)
 
     def edge_copy(side):
@@ -385,6 +405,12 @@
         edge_copy(side).start()
     links.fold_rim_start((1, 2), (0, 2), rim, fold_rim, fold_rim_sem)
 
+    def far_copy(n):
+        return links.far_copy(n, rim, margins, far_rows, far_blocks, far_sem)
+
+    for n in Links.FAR:
+        links.when_lat(Links.SHIFTS[n][0], lambda n=n: far_copy(n).start())
+
     for side in range(2):
         edge_copy(side).wait()
     for side in range(2):
@@ -408,6 +434,10 @@
                 links.fold_sent(s, lambda s=s, part=part: fold_cell_copy(s, part), True)
 
     links.fold_rim_finish((1, 2), (0, 2), rim, fold_rim, fold_rim_sem)
+    for n in Links.FAR:
+        links.when_lat(-Links.SHIFTS[n][0], lambda n=n: far_copy(n).wait_recv())
+    for n in Links.FAR:
+        links.when_lat(Links.SHIFTS[n][0], lambda n=n: far_copy(n).wait_send())
 
 
 def first_exchange_call(lon_size, lat_size, turn, collective_id):
@@ -421,24 +451,29 @@
             jax.ShapeDtypeStruct((2, 5, LEVELS, LANES), f32),
             jax.ShapeDtypeStruct((2, 5, 3, 2, LEVELS, LANES), f32),
             jax.ShapeDtypeStruct((2, 4, MARGIN, COLS), f32),
+            jax.ShapeDtypeStruct((2, 4, 8, COLS), f32),
+            jax.ShapeDtypeStruct((2, 2, 2, LEVELS, LANES), f32),
         ),
-        in_specs=[anywhere] * 3,
-        out_specs=(anywhere,) * 4,
-        scratch_shapes=[dma((2, 2))] * 5 + [dma((2, 2, 4))],
-        compiler_params=pltpu.CompilerParams(collective_id=collective_id, has_side_effects=True),
+        in_specs=[anywhere] * 4,
+        out_specs=(anywhere,) * 6,
+        scratch_shapes=[dma((2, 14))] + [dma((2, 2))] * 5 + [dma((2, 2, 4))],
+        compiler_params=pltpu.CompilerParams(
+            collective_id=collective_id, has_side_effects=True, vmem_limit_bytes=4 << 20
+        ),
         name="first_exchange",
     )
 
 
 def interior(
-    lon_size, lat_size, seam_ref, cells_in, edges, rim_in, bands, edges_in, fold_cells, fold_rim, rim_own, margins,
+    lon_size, lat_size, fold_ref, cells_in, edges, rim_in, bands, edges_in, fold_cells, fold_rim, rim_own, margins,
     centre, blocks, moved, done, means, mean_margins,
     cells, halo, face_west, flux_north, part, sums, ghost, ghost_margins, cell_sem, rim_sem, ghost_sem
 ):
     f32 = jnp.float32
     links = Links(lon_size, lat_size)
     lat = links.lat
-    count = links.meet(Links.SHIFTS)
+    near = [(n, Links.SHIFTS[n]) for n in Links.NEAR]
+    count = links.meet([shift for _, shift in near])
     filled = pltpu.make_async_copy(cells_in, cells.at[:, 3 : 3 + ROWS], cell_sem.at[0])
     south = pltpu.make_async_copy(bands.at[0], cells.at[:, 0:3], cell_sem.at[1])
     north = pltpu.make_async_copy(bands.at[1], cells.at[:, ROWS + 3 : ROWS + 6], cell_sem.at[2])
@@ -460,7 +495,7 @@
 
     @pl.when(links.top)
     def _():
-        turn_lanes, flip_rows, same_tile = turner(seam_ref)
+        turn_lanes, flip_rows, same_tile = turner(fold_ref)
 
         def image(tile):
             turned = [turn_lanes(tile(2 - n), tile(3 - n)) for n in range(3)]
@@ -549,16 +584,40 @@
             speed >= 0.0,
         )
 
-    filled.wait()
-
-    def north_face(face):
+
+    def unpack(r, _):
+        for f in range(5):
+            east = pltpu.roll(edges_in[0, f], LANES - 3 * r, 1)
+            west = pltpu.roll(edges_in[1, f], LANES - 3 - 3 * r, 1)
+            halo[f, r] = jnp.where(lane < LANES // 2, east, west)
+        return _
+
+    lax.fori_loop(0, ROWS, unpack, 0, unroll=16)
+
+    def rim_copy(n):
+        return links.rim_copy(n, rim_own, margins, centre, blocks, rim_sem)
+
+    pl.semaphore_wait(links.barrier, count)
+    for n, (a, b) in near:
+        links.when_lat(a, lambda n=n: rim_copy(n).start())
+
+    @pl.when(links.top)
+    def _():
+        for row in range(2):
+            for copy in ghost_copies(row):
+                copy.start()
+
+    def north_face(face, cells, first):
+        def at(f, row, t):
+            return cells[f, row - first, t]
+
         speeds = []
         for t in range(2):
             speed = (
                 0.5
-                * (cells[1, face + 2, t] + cells[1, face + 3, t])
-                * cells[4, face + 2, t]
-                * cells[4, face + 3, t]
+                * (at(1, face - 1, t) + at(1, face, t))
+                * at(4, face - 1, t)
+                * at(4, face, t)
             )
             flux_north[4, face, t] = speed
             speeds.append(
@@ -566,66 +625,34 @@
             )
         for f in range(4):
             for t in range(2):
-                q = [cells[f, face + n, t] for n in range(6)]
+                q = [at(f, face + n - 3, t) for n in range(6)]
                 e = [q[n + 1] - q[n] for n in range(5)]
                 flux_north[f, face, t] = weno_flux(*e, q[2], q[3], *speeds[t])
 
     def north_loop(face, _):
-        north_face(face)
+        north_face(face, cells_in, 0)
         return _
 
-    lax.fori_loop(3, 14, north_loop, 0)
-
-    def rim_copy(n):
-        return links.rim_copy(n, rim_own, margins, centre, blocks, rim_sem)
-
-    pl.semaphore_wait(links.barrier, count)
-    for n, (a, b) in enumerate(Links.SHIFTS):
-        links.when_lat(a, lambda n=n: rim_copy(n).start())
-
-    @pl.when(links.top)
-    def _():
-        for row in range(2):
-            for copy in ghost_copies(row):
-                copy.start()
-
-    first_lane = lane == 0
-    last_lane = lane == LANES - 1
-
-    def unpack(r, _):
-        for f in range(5):
-            east = pltpu.roll(edges_in[0, f], LANES - 3 * r, 1)
-            west = pltpu.roll(edges_in[1, f], LANES - 3 - 3 * r, 1)
-            halo[f, r] = jnp.where(lane < LANES // 2, east, west)
-        return _
-
-    lax.fori_loop(0, ROWS, unpack, 0)
-
-    def ahead_1(x):
-        turned = [pltpu.roll(v, LANES - 1, 1) for v in x]
-        return [jnp.where(last_lane, turned[(n + 1) % 3], turned[n]) for n in range(3)]
-
-    def ahead_2(x):
-        turned = [pltpu.roll(v, LANES - 2, 1) for v in x]
+    lax.fori_loop(3, 14, north_loop, 0, unroll=11)
+
+    def ahead(x, n, count=2):
         return [
-            jnp.where(lane >= LANES - 2, turned[(n + 1) % 3], turned[n]) for n in range(2)
+            pltpu.roll(jnp.where(lane < n, x[(t + 1) % 3], x[t]), LANES - n, 1)
+            for t in range(count)
         ]
 
-    def behind_1(x):
-        turned = [pltpu.roll(v, 1, 1) for v in x]
-        return [jnp.where(first_lane, turned[(n + 2) % 3], turned[n]) for n in range(2)]
-
-    def behind_2(x):
-        turned = [pltpu.roll(v, 2, 1) for v in x]
-        return [jnp.where(lane < 2, turned[(n + 2) % 3], turned[n]) for n in range(2)]
+    def behind(x, n):
+        return [
+            pltpu.roll(jnp.where(lane >= LANES - n, x[(t + 2) % 3], x[t]), n, 1) for t in range(2)
+        ]
 
     def east_loop(r, _):
-        wet = [cells[4, r + 3, 0], cells[4, r + 3, 1], halo[4, r]]
-        wet_next = ahead_1(wet)
+        wet = [cells_in[4, r, 0], cells_in[4, r, 1], halo[4, r]]
+        wet_next = ahead(wet, 1)
         gaps, nexts, firsts = [], [], []
         for f in range(4):
-            q = [cells[f, r + 3, 0], cells[f, r + 3, 1], halo[f, r]]
-            nxt = ahead_1(q)
+            q = [cells_in[f, r, 0], cells_in[f, r, 1], halo[f, r]]
+            nxt = ahead(q, 1, 3)
             firsts.append(q)
             nexts.append(nxt)
             gaps.append([nxt[n] - q[n] for n in range(3)])
@@ -633,28 +660,25 @@
         for t in range(2):
             speed = 0.5 * (firsts[0][t] + nexts[0][t]) * wet[t] * wet_next[t]
             speeds.append(speed)
-        behind = []
+        trails = []
 
         def difference(x, first):
-            turned = [pltpu.roll(v, 1, 1) for v in x]
-            return (
-                x[0] - jnp.where(first_lane, first, turned[0]),
-                x[1] - jnp.where(first_lane, turned[0], turned[1]),
-            )
+            west = behind([x[0], x[1], first], 1)
+            return x[0] - west[0], x[1] - west[1]
 
         def west_of(f):
-            return pltpu.roll(face_west[f], LANES - 3 * r, 1)
+            return pltpu.roll(face_west[f], LANES - 1 - 3 * r, 1)
 
         spread = difference(speeds, west_of(4))
         for t in range(2):
             part[4, r, t] = spread[t]
         for f in range(4):
             e = gaps[f]
-            em1 = behind_1(e)
-            em2 = behind_2(e)
-            ep1 = ahead_1(e)
-            ep2 = ahead_2(e)
-            behind.append(em1)
+            em1 = behind(e, 1)
+            em2 = behind(e, 2)
+            ep1 = ahead(e, 1)
+            ep2 = ahead(e, 2)
+            trails.append(em1)
             flux = [
                 weno_flux(
                     em2[t],
@@ -674,19 +698,20 @@
             for t in range(2):
                 part[f, r, t] = lost[t]
         for t in range(2):
-            part[5, r, t] = 0.8 * (gaps[3][t] + behind[3][t]) - 0.2 * (
-                gaps[2][t] + behind[2][t]
+            part[5, r, t] = 0.8 * (gaps[3][t] + trails[3][t]) - 0.2 * (
+                gaps[2][t] + trails[2][t]
             )
         return _
 
-    lax.fori_loop(0, ROWS, east_loop, 0)
-
+    lax.fori_loop(0, ROWS, east_loop, 0, unroll=4)
+
+    filled.wait()
     links.when_lat(-1, south.wait)
     links.when_lat(1, north.wait)
 
     def outer_loop(n, _):
-        north_face(n)
-        north_face(n + 14)
+        north_face(n, cells, -3)
+        north_face(n + 14, cells, -3)
         return _
 
     lax.fori_loop(0, 3, outer_loop, 0)
@@ -735,7 +760,7 @@
             done[1, t, pl.ds(r, LEVELS, stride=ROWS), :] = wet * (q[3] + rates[3])
         return _
 
-    lax.fori_loop(0, ROWS, combine, 0)
+    lax.fori_loop(0, ROWS, combine, 0, unroll=4)
 
     for t in range(2):
         lanes = slice(t * LANES, (t + 1) * LANES)
@@ -750,9 +775,9 @@
     mean_margins[0, 0], mean_margins[1, 0] = pack_margins(tiles)
 
     keep.wait()
-    for n, (a, b) in enumerate(Links.SHIFTS):
+    for n, (a, b) in near:
         links.when_lat(-a, lambda n=n: rim_copy(n).wait_recv())
-    for n, (a, b) in enumerate(Links.SHIFTS):
+    for n, (a, b) in near:
         links.when_lat(a, lambda n=n: rim_copy(n).wait_send())
 
     @pl.when(links.top)
@@ -786,7 +811,7 @@
             jax.ShapeDtypeStruct((2, 1, LEVELS, LANES), f32),
         ),
         in_specs=[pl.BlockSpec(memory_space=pltpu.SMEM)]
-        + [anywhere, vmem, vmem, anywhere, vmem, vmem, vmem, anywhere, anywhere],
+        + [vmem, vmem, vmem, anywhere, vmem, vmem, vmem, anywhere, anywhere],
         out_specs=(anywhere, anywhere, vmem, vmem, vmem, vmem),
         scratch_shapes=[
             pltpu.VMEM((5, ROWS + 6, 2, LEVELS, LANES), f32),
@@ -801,7 +826,9 @@
             dma((2, 14)),
             dma((2, 5)),
         ],
-        compiler_params=pltpu.CompilerParams(collective_id=collective_id, has_side_effects=True),
+        compiler_params=pltpu.CompilerParams(
+            collective_id=collective_id, has_side_effects=True, vmem_limit_bytes=12 << 20
+        ),
         name="interior",
     )
 
@@ -841,13 +868,15 @@
         in_specs=[anywhere] * 2,
         out_specs=(anywhere,) * 3,
         scratch_shapes=[dma((2, 14)), dma((2, 2, 4))],
-        compiler_params=pltpu.CompilerParams(collective_id=collective_id, has_side_effects=True),
+        compiler_params=pltpu.CompilerParams(
+            collective_id=collective_id, has_side_effects=True, vmem_limit_bytes=4 << 20
+        ),
         name="second_exchange",
     )
 
 
 def finish(
-    lat_size, seam_ref, centre_a, blocks_a, centre_b, blocks_b, fold_b, means, rim_own, moved, done_in,
+    lat_size, fold_ref, far_rows, far_blocks, centre_a, blocks_a, centre_b, blocks_b, fold_b, means, rim_own, moved, done_in,
     u_out, v_out, t_out, s_out, sea_out, zon_out, mer_out,
     wave, done, flat, tally, sems
 ):
@@ -866,19 +895,33 @@
     lane = lax.broadcasted_iota(jnp.int32, (LEVELS, LANES), 1)
     own_rows = slice(MARGIN, MARGIN + ROWS)
     row = lax.broadcasted_iota(jnp.int32, (WIDE, width), 0) + (lat * ROWS - MARGIN)
+
+    def side_tile(from_east, from_west, n, part):
+        lead = MARGIN * (2 * (n % 2) + part)
+        if lead:
+            from_east = pltpu.roll(from_east, LANES - lead, 1)
+        from_west = pltpu.roll(from_west, LANES - MARGIN - lead, 1)
+        return jnp.where(lane < LANES // 2, from_east, from_west)
+
     sources = ((0, 1), (1, 0), (1, 1), (2, 0), (2, 1), (3, 0), (3, 1), (4, 0))
     for f in range(6):
         centre, blocks, n = (centre_a, blocks_a, f) if f < 4 else (centre_b, blocks_b, f - 4)
         wave[f, :, 0:COLS] = centre[n]
-        for i, (block, part) in enumerate(sources):
-            lead = MARGIN * (2 * (n % 2) + part)
-            from_east = blocks[block, 0, n // 2]
-            if lead:
-                from_east = pltpu.roll(from_east, LANES - lead, 1)
-            from_west = pltpu.roll(blocks[block, 1, n // 2], LANES - MARGIN - lead, 1)
-            wave[f, 8 * i : 8 * i + 8, COLS:width] = jnp.where(
-                lane < LANES // 2, from_east, from_west
+        for i in range(8):
+            block, part = sources[i]
+            wave[f, 8 * i : 8 * i + 8, COLS:width] = side_tile(
+                blocks[block, 0, n // 2], blocks[block, 1, n // 2], n, part
             )
+    for side, rows, part, here in ((0, 0, 1, lat > 1), (1, WIDE - 8, 0, lat < lat_size - 2)):
+
+        @pl.when(here)
+        def _():
+            for f in range(4):
+                wave[f, rows : rows + 8, 0:COLS] = far_rows[side, f]
+                wave[f, rows : rows + 8, COLS:width] = side_tile(
+                    far_blocks[side, 0, f // 2], far_blocks[side, 1, f // 2], f, part
+                )
+
     for f in range(2):
         wave[MEANZ + f, own_rows, 0:COLS] = means[f]
     for n, empty in ((0, MARGIN), (1, 8)):
@@ -888,7 +931,7 @@
             wave[0:6, 0:empty] = jnp.zeros((6, empty, width), f32)
 
     def unfold(ghost_tiles):
-        turn_lanes, flip_rows, same_tile = turner(seam_ref)
+        turn_lanes, flip_rows, same_tile = turner(fold_ref)
 
         def mean(n, _):
             for to, source in ghost_tiles:
@@ -925,31 +968,32 @@
         return pltpu.roll(x, width - 1, 1) - pltpu.roll(x, 1, 1)
 
     def north_difference(x):
-        return pltpu.roll(x, WIDE - 1, 0) - pltpu.roll(x, 1, 0)
-
-    def substep(n, _):
-        thick = wave[TALLY]
-        wet = wave[6]
-        zonal = wave[ZON]
-        merid = wave[MER]
+        return pltpu.roll(x, x.shape[0] - 1, 0) - pltpu.roll(x, 1, 0)
+
+    def substep(rows):
+        thick = wave[TALLY, rows]
+        wet = wave[6, rows]
+        zonal = wave[ZON, rows]
+        merid = wave[MER, rows]
         level_next = wet * (
-            wave[SEA] - (east_difference(thick * zonal) + north_difference(thick * merid))
+            wave[SEA, rows] - (east_difference(thick * zonal) + north_difference(thick * merid))
         )
-        turn_rate = wave[7]
-        wave[SEA] = level_next
-        wave[ZON] = wet * (
+        turn_rate = wave[7, rows]
+        wave[SEA, rows] = level_next
+        wave[ZON, rows] = wet * (
             zonal
             - (0.5 * WAVE_MOMENTUM) * east_difference(level_next)
-            + (turn_rate * merid + wave[MEANZ])
+            + (turn_rate * merid + wave[MEANZ, rows])
         )
-        wave[MER] = wet * (
+        wave[MER, rows] = wet * (
             merid
             - (0.5 * WAVE_MOMENTUM) * north_difference(level_next)
-            + (wave[MEANM] - turn_rate * zonal)
+            + (wave[MEANM, rows] - turn_rate * zonal)
         )
-        return _
-
-    lax.fori_loop(0, SUBSTEPS, substep, 0)
+
+    for stage in range(SUBSTEPS // 4):
+        rows = slice(8 * stage, WIDE - 8 * stage)
+        lax.fori_loop(0, 4, lambda n, _: (substep(rows), _)[1], 0)
 
     for f, ref in enumerate((sea_out, zon_out, mer_out)):
         copy = pltpu.make_async_copy(wave.at[f, own_rows, 0:COLS], ref, sems.at[8 + f])
@@ -972,7 +1016,7 @@
                 )
         return _
 
-    lax.fori_loop(0, ROWS, last, 0)
+    lax.fori_loop(0, ROWS, last, 0, unroll=16)
 
     for f, ref in ((0, u_out), (1, v_out)):
         for t in range(2):
@@ -993,7 +1037,7 @@
     return pl.pallas_call(
         functools.partial(finish, lat_size),
         out_shape=(deep,) * 4 + (flat,) * 3,
-        in_specs=[pl.BlockSpec(memory_space=pltpu.SMEM)] + [vmem] * 9,
+        in_specs=[pl.BlockSpec(memory_space=pltpu.SMEM)] + [vmem] * 11,
         out_specs=(anywhere,) * 7,
         scratch_shapes=[
             pltpu.VMEM((8, WIDE, COLS + LANES), f32),
@@ -1002,6 +1046,7 @@
             pltpu.VMEM((2, ROWS, LANES), f32),
             pltpu.SemaphoreType.DMA((11,)),
         ],
+        compiler_params=pltpu.CompilerParams(vmem_limit_bytes=12 << 20),
         name="finish",
     )(*arguments)
 
@@ -1009,18 +1054,19 @@
 def on_device(lon_size, lat_size, *arguments):
     *fields, sea, zon, mer, tally, seam = arguments
     deep = [x.reshape(LEVELS * ROWS, COLS) for x in fields]
-    turn = lax.rem(lax.shift_right_logical(seam[0], 8) + lax.axis_index("lon"), lon_size)
-    cells, edges, rim_own, margins = prepare_call(*deep, sea, zon, mer, tally)
-    bands, edges_in, fold_cells, fold_a = lax.switch(
+    cells, edges, rim_own, margins, fold = prepare_call(lon_size, *deep, sea, zon, mer, tally, seam)
+    turn = fold[0]
+    bands, edges_in, fold_cells, fold_a, far_rows, far_blocks = lax.switch(
         turn,
         [first_exchange_call(lon_size, lat_size, n, n) for n in range(lon_size)],
         cells,
         edges,
         rim_own,
+        margins,
     )
     centre_a, blocks_a, moved, done, means, mean_margins = interior_call(
         lon_size, lat_size, 2 * lon_size
-    )(seam, cells, edges, rim_own, bands, edges_in, fold_cells, fold_a, rim_own, margins)
+    )(fold, cells, edges, rim_own, bands, edges_in, fold_cells, fold_a, rim_own, margins)
     centre_b, blocks_b, fold_b = lax.switch(
         turn,
         [second_exchange_call(lon_size, lat_size, n, lon_size + n) for n in range(lon_size)],
@@ -1028,7 +1074,8 @@
         mean_margins,
     )
     out = finish_call(
-        lat_size, seam, centre_a, blocks_a, centre_b, blocks_b, fold_b, means, rim_own, moved, done
+        lat_size, fold, far_rows, far_blocks, centre_a, blocks_a, centre_b, blocks_b, fold_b, means, rim_own,
+        moved, done
     )
     return tuple(x.reshape(LEVELS, ROWS, COLS) for x in out[:4]) + tuple(out[4:])
 

time: 50.9 us -> 47.7 us (0.937)
  Pallas kernels: 47.3 us -> 45.9 us
  between operations: 1.52 us -> 0.88 us
  local copies, waits for them, and re-layouts: 1.19 us -> 0.65 us
    pallas_call x1, Pallas kernels: 17.2 us -> 7.61 us  [on_device(): interior_call(lon_size, lat_size, 2 * lon_size)]
    pallas_call x1, Pallas kernels: 13.6 us -> 20.6 us  [on_device(): lax.switch(turn, [first_exchange_call(lon_size, lat_size, n, n) for n in...]
    pallas_call x1, Pallas kernels: 7.67 us -> 11.1 us  [on_device(): lax.switch(turn, [second_exchange_call(lon_size, lat_size, n, lon_size +...]
    pallas_call x1, Pallas kernels: 3.26 us -> 1.91 us  [prepare_call(): pl.pallas_call(functools.partial(prepare, lon_size), out_shape=(jax.Shape...]
    pallas_call x1, Pallas kernels: 5.6 us -> 4.65 us  [finish_call(): pl.pallas_call(functools.partial(finish, lat_size), out_shape=(deep,) * 4...]
    slice x1 -> x0, local copies, waits for them, and re-layouts: 0.51 us -> none  [on_device(): seam[0]]
where the time goes in v1:
time: 47.7 us; the launch traced here: 47.5 us
  Pallas kernels  45.9 us (96%)
  between operations  0.88 us (2%)
  local copies, waits for them, and re-layouts  0.65 us (1%)
    pallas_call x1, Pallas kernels, on_device(): lax.switch(turn, [first_exchange_call(lon_size, lat_size, n, n) for n in...  20.6 us
    pallas_call x1, Pallas kernels, on_device(): lax.switch(turn, [second_exchange_call(lon_size, lat_size, n, lon_size +...  11.1 us
    pallas_call x1, Pallas kernels, on_device(): interior_call(lon_size, lat_size, 2 * lon_size)  7.61 us
    pallas_call x1, Pallas kernels, finish_call(): pl.pallas_call(functools.partial(finish, lat_size), out_shape=(deep,) * 4...  4.65 us
    pallas_call x1, Pallas kernels, prepare_call(): pl.pallas_call(functools.partial(prepare, lon_size), out_shape=(jax.Shape...  1.91 us

profile of v1, /device:TPU:7, one launch (start us, length us, event | category | flops | bytes accessed | tf_op | source)
XLA Modules:
  0.0 47.5 jit_solution(2517680695232790600)
XLA Ops:
  0.6 1.9 %prepare.1 = (f32[5,16,2,8,128]{4,3,2,1,0:T(8,128)S(1)}, f32[2,5,8,128]{3,2,1,0:T(8,128)S(1)}, f32[4,16,256]{2,1,0:T(8,128)S(1)}, f32[2,2,8,128]{3,2,1,0:T(8,128)S(1)}, s32[2]{0:T(128)}) custom-call(f32[128,256]{1,0:T(8,128)} %bitcast.11, f32[128,256]{1,0:T(8,128)} %bitcast.12, f32[128,256]{1,0:T(8,128)} %bitcast.13, f32[128,256]{1,0:T(8,128)} %bitcast.14, ...), custom_call_target="tpu_custom_call" | custom-call | tf_op jit(solution)/shard_map/prepare/pallas_call | solution.py:147
  2.6 0.0 copy-start
  2.6 0.6 %copy-done = s32[2]{0:T(128)S(1)} copy-done((s32[2]{0:T(128)S(1)}, s32[2]{0:T(128)}, u32[]{:S(2)}) %copy-start) | copy-done | bytes 32
  3.3 20.6 %conditional.2 = ((f32[2,5,3,2,8,128]{5,4,3,2,1,0:T(8,128)S(1)}, f32[2,5,8,128]{3,2,1,0:T(8,128)S(1)}, f32[2,5,3,2,8,128]{5,4,3,2,1,0:T(8,128)S(1)}, f32[2,4,24,...) conditional(s32[]{:T(128)} %bitcast.4, ...), branch_computations={%region_0.0_spmd, %region_1.0_spmd, %region_2.0_spmd, %region_3.0_... | conditional | bytes 8 | solution.py:1059
  3.3 20.6 %first_exchange.16 = (f32[2,5,3,2,8,128]{5,4,3,2,1,0:T(8,128)S(1)}, f32[2,5,8,128]{3,2,1,0:T(8,128)S(1)}, f32[2,5,3,2,8,128]{5,4,3,2,1,0:T(8,128)S(1)}, f32[2,4,...) custom-call(f32[5,16,2,8,128]{4,3,2,1,0:T(8,128)S(1)} %get-tuple-element.192.cells, ...), custom_call_target="tpu_custom_call" | custom-call | tf_op jit(solution)/shard_map/cond/branch_0_fun/first_exchange/pallas_call | solution.py:1059
  23.9 7.6 %interior.1 = (f32[4,64,256]{2,1,0:T(8,128)S(1)}, f32[5,2,2,8,128]{4,3,2,1,0:T(8,128)S(1)}, f32[2,16,2,8,128]{4,3,2,1,0:T(8,128)S(1)}, f32[2,2,128,128]{3,2,1,0:...) custom-call(s32[2]{0:T(128)S(1)} %copy-done, ...), custom_call_target="tpu_custom_call" | custom-call | tf_op jit(solution)/shard_map/interior/pallas_call | solution.py:1067
  31.5 11.2 %conditional.3 = ((f32[2,64,256]{2,1,0:T(8,128)S(1)}, f32[5,2,1,8,128]{4,3,2,1,0:T(8,128)S(1)}, f32[4,2,24,256]{3,2,1,0:T(8,128)S(1)})) conditional(s32[]{:T(128)} %bitcast.4, (f32[2,16,256]{2,1,0:T(8,128)S(1)}, f32[2,1,8,128]{3,2,1,0:T(8,128)S(1)}) %tuple.105, (f32[2,16,256]{2,1,0:T(8,128)S(1)}, ...), branch_computations={%region_16.0_spmd, %region_17.0_spmd, %region_18.0_spmd, %region_1... | conditional | bytes 8 | solution.py:1070
  31.5 11.1 %second_exchange.16 = (f32[2,64,256]{2,1,0:T(8,128)S(1)}, f32[5,2,1,8,128]{4,3,2,1,0:T(8,128)S(1)}, f32[4,2,24,256]{3,2,1,0:T(8,128)S(1)}) custom-call(f32[2,16,256]{2,1,0:T(8,128)S(1)} %get-tuple-element.256.means, f32[2,1,8,128]{3,2,1,0:T(8,128)S(1)} %get-tuple-element.257.margins), custom_call_target="tpu_custom_call" | custom-call | tf_op jit(solution)/shard_map/cond/branch_0_fun/second_exchange/pallas_call | solution.py:1070
  42.7 4.6 %finish.1 = (f32[128,256]{1,0:T(8,128)}, f32[128,256]{1,0:T(8,128)}, f32[128,256]{1,0:T(8,128)}, f32[128,256]{1,0:T(8,128)}, f32[16,256]{1,0:T(8,128)}, /*index=5*/f32[16,256]{1,0:T(8,128)}, f32[16,256]{1,0:T(8,128)}) custom-call(s32[2]{0:T(128)S(1)} %copy-done, f32[2,4,8,256]{3,2,1,0:T(8,128)S(1)} %get-tuple-element.327.far_rows, ...), custom_call_target="tpu_custom_call" | custom-call | tf_op jit(solution)/shard_map/finish/pallas_call | solution.py:1037
Async XLA Ops:
  2.6 0.7 %copy-start = (s32[2]{0:T(128)S(1)}, s32[2]{0:T(128)}, u32[]{:S(2)}) copy-start(s32[2]{0:T(128)} %get-tuple-element.322.fold_ref) | copy-start | bytes 28

commit v2 on v1

--- a/solution.py
+++ b/solution.py
@@ -385,6 +385,21 @@
     def fold_cell_copy(s, part):
         return links.copy(*part(s), {"lat": links.lat, "lon": links.fold_peer(s)})
 
+    for side in range(2):
+
+        def send(side=side):
+            for copy in band_copies(side):
+                copy.start()
+
+        links.when_lat(1 - 2 * side, send)
+    for side in range(2):
+        edge_copy(side).start()
+    def far_copy(n):
+        return links.far_copy(n, rim, margins, far_rows, far_blocks, far_sem)
+
+    for n in Links.FAR:
+        links.when_lat(Links.SHIFTS[n][0], lambda n=n: far_copy(n).start())
+
     @pl.when(links.top)
     def _():
         for s in (1, 2):
@@ -394,22 +409,7 @@
                     s, lambda s=s, part=part: fold_cell_copy(s, part), a, b, sem.at[1], True
                 )
 
-    for side in range(2):
-
-        def send(side=side):
-            for copy in band_copies(side):
-                copy.start()
-
-        links.when_lat(1 - 2 * side, send)
-    for side in range(2):
-        edge_copy(side).start()
     links.fold_rim_start((1, 2), (0, 2), rim, fold_rim, fold_rim_sem)
-
-    def far_copy(n):
-        return links.far_copy(n, rim, margins, far_rows, far_blocks, far_sem)
-
-    for n in Links.FAR:
-        links.when_lat(Links.SHIFTS[n][0], lambda n=n: far_copy(n).start())
 
     for side in range(2):
         edge_copy(side).wait()
@@ -993,7 +993,7 @@
 
     for stage in range(SUBSTEPS // 4):
         rows = slice(8 * stage, WIDE - 8 * stage)
-        lax.fori_loop(0, 4, lambda n, _: (substep(rows), _)[1], 0)
+        lax.fori_loop(0, 4, lambda n, _: (substep(rows), _)[1], 0, unroll=2)
 
     for f, ref in enumerate((sea_out, zon_out, mer_out)):
         copy = pltpu.make_async_copy(wave.at[f, own_rows, 0:COLS], ref, sems.at[8 + f])

time: 47.7 us -> 44.6 us (0.935)
  Pallas kernels: 45.9 us -> 42.6 us
    pallas_call x1, Pallas kernels: 20.6 us -> 16.2 us  [on_device(): lax.switch(turn, [first_exchange_call(lon_size, lat_size, n, n) for n in...]
    pallas_call x1, Pallas kernels: 7.61 us -> 10.7 us  [on_device(): interior_call(lon_size, lat_size, 2 * lon_size)]
    pallas_call x1, Pallas kernels: 11.1 us -> 9.23 us  [on_device(): lax.switch(turn, [second_exchange_call(lon_size, lat_size, n, lon_size +...]
where the time goes in v2:
time: 44.6 us; the launch traced here: 44.2 us
  Pallas kernels  42.6 us (96%)
  between operations  0.88 us (2%)
  local copies, waits for them, and re-layouts  0.65 us (1%)
    pallas_call x1, Pallas kernels, on_device(): lax.switch(turn, [first_exchange_call(lon_size, lat_size, n, n) for n in...  16.2 us
    pallas_call x1, Pallas kernels, on_device(): interior_call(lon_size, lat_size, 2 * lon_size)  10.7 us
    pallas_call x1, Pallas kernels, on_device(): lax.switch(turn, [second_exchange_call(lon_size, lat_size, n, lon_size +...  9.23 us
    pallas_call x1, Pallas kernels, finish_call(): pl.pallas_call(functools.partial(finish, lat_size), out_shape=(deep,) * 4...  4.57 us
    pallas_call x1, Pallas kernels, prepare_call(): pl.pallas_call(functools.partial(prepare, lon_size), out_shape=(jax.Shape...  1.91 us

profile of v2, /device:TPU:7, one launch (start us, length us, event | category | flops | bytes accessed | tf_op | source)
XLA Modules:
  0.0 44.2 jit_solution(158343992997697588)
XLA Ops:
  0.6 1.9 %prepare.1 = (f32[5,16,2,8,128]{4,3,2,1,0:T(8,128)S(1)}, f32[2,5,8,128]{3,2,1,0:T(8,128)S(1)}, f32[4,16,256]{2,1,0:T(8,128)S(1)}, f32[2,2,8,128]{3,2,1,0:T(8,128)S(1)}, s32[2]{0:T(128)}) custom-call(f32[128,256]{1,0:T(8,128)} %bitcast.11, f32[128,256]{1,0:T(8,128)} %bitcast.12, f32[128,256]{1,0:T(8,128)} %bitcast.13, f32[128,256]{1,0:T(8,128)} %bitcast.14, ...), custom_call_target="tpu_custom_call" | custom-call | tf_op jit(solution)/shard_map/prepare/pallas_call | solution.py:147
  2.6 0.0 copy-start
  2.6 0.6 %copy-done = s32[2]{0:T(128)S(1)} copy-done((s32[2]{0:T(128)S(1)}, s32[2]{0:T(128)}, u32[]{:S(2)}) %copy-start) | copy-done | bytes 32
  3.3 16.2 %conditional.2 = ((f32[2,5,3,2,8,128]{5,4,3,2,1,0:T(8,128)S(1)}, f32[2,5,8,128]{3,2,1,0:T(8,128)S(1)}, f32[2,5,3,2,8,128]{5,4,3,2,1,0:T(8,128)S(1)}, f32[2,4,24,...) conditional(s32[]{:T(128)} %bitcast.4, ...), branch_computations={%region_0.0_spmd, %region_1.0_spmd, %region_2.0_spmd, %region_3.0_... | conditional | bytes 8 | solution.py:1059
  3.3 16.2 %first_exchange.25 = (f32[2,5,3,2,8,128]{5,4,3,2,1,0:T(8,128)S(1)}, f32[2,5,8,128]{3,2,1,0:T(8,128)S(1)}, f32[2,5,3,2,8,128]{5,4,3,2,1,0:T(8,128)S(1)}, f32[2,4,...) custom-call(f32[5,16,2,8,128]{4,3,2,1,0:T(8,128)S(1)} %get-tuple-element.228.cells, ...), custom_call_target="tpu_custom_call" | custom-call | tf_op jit(solution)/shard_map/cond/branch_9_fun/first_exchange/pallas_call | solution.py:1059
  19.5 10.7 %interior.1 = (f32[4,64,256]{2,1,0:T(8,128)S(1)}, f32[5,2,2,8,128]{4,3,2,1,0:T(8,128)S(1)}, f32[2,16,2,8,128]{4,3,2,1,0:T(8,128)S(1)}, f32[2,2,128,128]{3,2,1,0:...) custom-call(s32[2]{0:T(128)S(1)} %copy-done, ...), custom_call_target="tpu_custom_call" | custom-call | tf_op jit(solution)/shard_map/interior/pallas_call | solution.py:1067
  30.2 9.3 %conditional.3 = ((f32[2,64,256]{2,1,0:T(8,128)S(1)}, f32[5,2,1,8,128]{4,3,2,1,0:T(8,128)S(1)}, f32[4,2,24,256]{3,2,1,0:T(8,128)S(1)})) conditional(s32[]{:T(128)} %bitcast.4, (f32[2,16,256]{2,1,0:T(8,128)S(1)}, f32[2,1,8,128]{3,2,1,0:T(8,128)S(1)}) %tuple.105, (f32[2,16,256]{2,1,0:T(8,128)S(1)}, ...), branch_computations={%region_16.0_spmd, %region_17.0_spmd, %region_18.0_spmd, %region_1... | conditional | bytes 8 | solution.py:1070
  30.2 9.2 %second_exchange.25 = (f32[2,64,256]{2,1,0:T(8,128)S(1)}, f32[5,2,1,8,128]{4,3,2,1,0:T(8,128)S(1)}, f32[4,2,24,256]{3,2,1,0:T(8,128)S(1)}) custom-call(f32[2,16,256]{2,1,0:T(8,128)S(1)} %get-tuple-element.274.means, f32[2,1,8,128]{3,2,1,0:T(8,128)S(1)} %get-tuple-element.275.margins), custom_call_target="tpu_custom_call" | custom-call | tf_op jit(solution)/shard_map/cond/branch_9_fun/second_exchange/pallas_call | solution.py:1070
  39.5 4.6 %finish.1 = (f32[128,256]{1,0:T(8,128)}, f32[128,256]{1,0:T(8,128)}, f32[128,256]{1,0:T(8,128)}, f32[128,256]{1,0:T(8,128)}, f32[16,256]{1,0:T(8,128)}, /*index=5*/f32[16,256]{1,0:T(8,128)}, f32[16,256]{1,0:T(8,128)}) custom-call(s32[2]{0:T(128)S(1)} %copy-done, f32[2,4,8,256]{3,2,1,0:T(8,128)S(1)} %get-tuple-element.327.far_rows, ...), custom_call_target="tpu_custom_call" | custom-call | tf_op jit(solution)/shard_map/finish/pallas_call | solution.py:1037
Async XLA Ops:
  2.6 0.7 %copy-start = (s32[2]{0:T(128)S(1)}, s32[2]{0:T(128)}, u32[]{:S(2)}) copy-start(s32[2]{0:T(128)} %get-tuple-element.322.fold_ref) | copy-start | bytes 28
